TPU v7x, 32 devices: a whole 2x2x4 slice. The times are simulated.
32 devices in a mesh: dp: 8 (over z, x), expert: 4 (over y, core).
Axes of the slice: x: 2, y: 2, z: 4, core: 2. Of those that a mesh axis runs over, the one named last changes fastest.
Arguments:
- tokens: bfloat16 [8192, 768], P(('dp', 'expert')), may hold values from -6 to 6
- expert_ids: int32 [8192, 2], P(('dp', 'expert')), may hold values from 0 to 15, all different within a row; in each aligned block of 256 rows (0 to 255, 256 to 511, ...) at most 64 rows name the same one
- gate_fixed: int32 [8192, 2], P(('dp', 'expert')), may hold values from 8192 to 65535
- cotangent: bfloat16 [8192, 768], P(('dp', 'expert')), may hold values from -6 to 6
- w_gate: bfloat16 [16, 768, 384], P('expert'), may hold values from -0.21875 to 0.21875
- w_up: bfloat16 [16, 768, 384], P('expert'), may hold values from -0.21875 to 0.21875
- w_down: bfloat16 [16, 768, 384], P('expert'), may hold values from -0.3125 to 0.3125
Outputs:
- layer_out: bfloat16 [8192, 768], P(('dp', 'expert'))
- input_grad: bfloat16 [8192, 768], P(('dp', 'expert'))
- grad_gate: float32 [16, 768, 384], P('expert', 'dp')
- grad_up: float32 [16, 768, 384], P('expert', 'dp')
- grad_down: float32 [16, 768, 384], P('expert', 'dp')
Inputs may be any that keep to these rules, and one draw needn't show every extreme that they name: `expert_ids`: A row names 2 different experts. In each aligned block of 256 rows (the rows of one device) no expert is named by more than 64 rows, and in some block one expert is named by exactly 64 rows.
All inputs are finite; a program needn't handle non-finite values.
Results may differ from a plain program's by a relative error of at most 0.015.
Values may be sent and summed in bfloat16 or wider, within the bound.
A program may use at most 64 MiB of HBM per device.

v0:
```python
import jax
import jax.numpy as jnp
from jax import lax
from jax.sharding import PartitionSpec as P


def expert_forward(rows_in, w_gate, w_up, w_down):
    pre_gate = jnp.einsum("erd,edf->erf", rows_in, w_gate, preferred_element_type=jnp.float32)
    pre_up = jnp.einsum("erd,edf->erf", rows_in, w_up, preferred_element_type=jnp.float32)
    sigmoid_gate = jax.nn.sigmoid(pre_gate)
    activated = pre_gate * sigmoid_gate
    hidden = (activated * pre_up).astype(jnp.bfloat16)
    outputs = jnp.einsum("erf,edf->erd", hidden, w_down, preferred_element_type=jnp.float32).astype(
        jnp.bfloat16
    )
    return (outputs, (pre_gate, pre_up, sigmoid_gate, activated, hidden))


def expert_backward(rows_in, grads_in, saved_state, w_gate, w_up, w_down, grad_scale):
    pre_gate, pre_up, sigmoid_gate, activated, hidden = saved_state
    hidden_grad = jnp.einsum("erd,edf->erf", grads_in, w_down, preferred_element_type=jnp.float32)
    gate_grad = (
        hidden_grad * pre_up * sigmoid_gate * (1.0 + pre_gate * (1.0 - sigmoid_gate))
    ).astype(jnp.bfloat16)
    up_grad = (hidden_grad * activated).astype(jnp.bfloat16)
    entry_grad = (
        jnp.einsum("erf,edf->erd", gate_grad, w_gate, preferred_element_type=jnp.float32)
        + jnp.einsum("erf,edf->erd", up_grad, w_up, preferred_element_type=jnp.float32)
    ).astype(jnp.bfloat16)
    weight_gate = (
        jnp.einsum("erd,erf->edf", rows_in, gate_grad, preferred_element_type=jnp.float32)
        * grad_scale
    )
    weight_up = (
        jnp.einsum("erd,erf->edf", rows_in, up_grad, preferred_element_type=jnp.float32)
        * grad_scale
    )
    weight_down = (
        jnp.einsum("erd,erf->edf", grads_in, hidden, preferred_element_type=jnp.float32)
        * grad_scale
    )
    return (entry_grad, weight_gate, weight_up, weight_down)


def shards(tokens, expert_ids, gate_fixed, cotangent, w_gate, w_up, w_down):
    peer_count = lax.axis_size("expert")
    replicas = lax.axis_size("dp")
    local_experts = w_gate.shape[0]
    tok_rows = expert_ids.shape[0]
    top_count = expert_ids.shape[1]
    d_model = tokens.shape[1]
    experts_all = local_experts * peer_count
    entries = tok_rows * top_count
    capacity = entries * 2 // experts_all
    slots_all = experts_all * capacity
    grad_scale = float(tok_rows * replicas * top_count // local_experts) ** (-0.5)
    flat_ids = expert_ids.reshape(entries)
    onehot = (flat_ids[:, None] == jnp.arange(experts_all, dtype=jnp.int32)[None, :]).astype(
        jnp.int32
    )
    slot_rank = jnp.sum((jnp.cumsum(onehot, axis=0) - 1) * onehot, axis=1)
    owner_dev = flat_ids // local_experts
    within = flat_ids % local_experts
    slot_index = (within * peer_count + owner_dev) * capacity + slot_rank
    source = (
        jnp.full((slots_all,), entries, jnp.int32)
        .at[slot_index]
        .set(jnp.arange(entries, dtype=jnp.int32))
    )
    is_valid = source < entries
    token_of = jnp.where(is_valid, source // top_count, 0)
    gate_values = gate_fixed.reshape(entries).astype(jnp.float32) / 65536.0
    slot_gate = jnp.where(is_valid, gate_values[jnp.minimum(source, entries - 1)], 0.0)
    send_rows = jnp.where(is_valid[:, None], tokens[token_of], jnp.zeros((), jnp.bfloat16))
    send_rows = send_rows.reshape(local_experts, peer_count * capacity, d_model)
    send_grads = (slot_gate[:, None] * cotangent[token_of].astype(jnp.float32)).astype(jnp.bfloat16)
    send_grads = send_grads.reshape(local_experts, peer_count * capacity, d_model)
    rows_in = lax.all_to_all(send_rows, "expert", split_axis=1, concat_axis=1, tiled=True)
    outputs, saved_state = expert_forward(rows_in, w_gate, w_up, w_down)
    back_out = lax.all_to_all(outputs, "expert", split_axis=1, concat_axis=1, tiled=True)
    grads_in = lax.all_to_all(send_grads, "expert", split_axis=1, concat_axis=1, tiled=True)
    entry_grad, weight_gate, weight_up, weight_down = expert_backward(
        rows_in, grads_in, saved_state, w_gate, w_up, w_down, grad_scale
    )
    back_in = lax.all_to_all(entry_grad, "expert", split_axis=1, concat_axis=1, tiled=True)

    def combine(returned, weights):
        picked = returned.reshape(slots_all, d_model)[slot_index].astype(jnp.float32)
        summed = jnp.sum((weights[:, None] * picked).reshape(tok_rows, top_count, d_model), axis=1)
        return summed.astype(jnp.bfloat16)

    layer_out = combine(back_out, gate_values)
    input_grad = combine(back_in, jnp.ones_like(gate_values))
    grad_gate, grad_up, grad_down = (
        lax.psum_scatter(
            weight_gate.astype(jnp.bfloat16), "dp", scatter_dimension=1, tiled=True
        ).astype(jnp.float32),
        lax.psum_scatter(
            weight_up.astype(jnp.bfloat16), "dp", scatter_dimension=1, tiled=True
        ).astype(jnp.float32),
        lax.psum_scatter(
            weight_down.astype(jnp.bfloat16), "dp", scatter_dimension=1, tiled=True
        ).astype(jnp.float32),
    )
    return (layer_out, input_grad, grad_gate, grad_up, grad_down)


def solution(mesh):
    return jax.shard_map(
        shards,
        mesh=mesh,
        in_specs=(
            P(("dp", "expert"), None),
            P(("dp", "expert"), None),
            P(("dp", "expert"), None),
            P(("dp", "expert"), None),
            P("expert", None, None),
            P("expert", None, None),
            P("expert", None, None),
        ),
        out_specs=(
            P(("dp", "expert"), None),
            P(("dp", "expert"), None),
            P("expert", "dp", None),
            P("expert", "dp", None),
            P("expert", "dp", None),
        ),
        check_vma=False,
    )
```

profile of v0, /device:TPU:0, one launch (start us, length us, event | category | flops | bytes accessed | tf_op | source)
XLA Modules:
  0.0 315.9 jit_solution(13793462235881466038)
XLA Ops:
  7.2 0.0 copy-start
  7.2 1.0 copy.44
  8.1 0.1 eq.31
  8.3 0.1 eq.27
  8.4 0.1 reshape.196
  8.6 0.7 convert_multiply_fusion
  9.3 0.1 copy.43
  9.4 0.1 div.43
  9.6 1.2 reduce-window.6
  10.7 0.2 slice_reduce_fusion
  11.0 0.1 fusion.3
  11.1 2.4 scatter_custom_fusion
  13.6 0.0 copy-start.1
  13.6 6.9 %gather_fusion.2 = f32[1024]{0:T(1024)S(1)} fusion(f32[512]{0:T(512)S(1)} %div.43, s32[1024]{0:T(1024)S(1)} %fusion.8), kind=kCustom, calls=%fused_computation.2 | custom fusion | bytes 12288 | tf_op jit(solution)/shard_map/gather | solution.py:73
  20.5 0.2 copy.48
  20.7 0.0 copy-done.1
  20.7 5.2 %gather_fusion = bf16[1024,768]{1,0:T(8,128)(2,1)} fusion(bf16[256,768]{1,0:T(8,128)(2,1)S(1)} %copy-done.1, s32[1024]{0:T(1024)S(1)} %fusion.7), kind=kCustom, calls=%fused_computation | custom fusion | bytes 3149824 | tf_op jit(solution)/shard_map/gather | solution.py:74
  25.9 3.8 %copy_select_fusion = bf16[4,256,768]{2,0,1:T(4,128)(2,1)} fusion(bf16[4,256,768]{2,1,0:T(8,128)(2,1)} %bitcast.43, pred[4,256]{0,1:T(8,128)(4,1)S(1)} %copy.48), kind=kLoop, calls=%fused_computation.13 | loop fusion | flops 786432 | bytes 3146752 | tf_op jit(solution)/shard_map/jit(_where)/select_n | solution.py:74
  29.8 4.5 %all-to-all-start = ((bf16[4,256,768]{2,0,1:T(4,128)(2,1)}), bf16[4,256,768]{2,0,1:T(4,128)(2,1)}, u32[]{:S(2)}, u32[]{:S(2)}) async-start(bf16[4,256,768]{2,0,1:T(4,128)(2,1)} %copy_select_fusion), calls=%async_computation | async-start | bytes 3145728 | tf_op jit(solution)/shard_map/all_to_all | solution.py:78
  34.3 0.1 copy.55
  34.4 5.2 %gather_fusion.3 = bf16[1024,768]{1,0:T(8,128)(2,1)} fusion(bf16[256,768]{1,0:T(8,128)(2,1)S(1)} %copy-done.2, s32[1024]{0:T(1024)S(1)} %fusion.7), kind=kCustom, calls=%fused_computation.3 | custom fusion | bytes 3149824 | tf_op jit(solution)/shard_map/gather | solution.py:76
  39.6 1.7 convert.3
  41.3 3.2 %fusion = bf16[4,256,768]{2,0,1:T(4,128)(2,1)} fusion(f32[4,256,768]{2,1,0:T(8,128)S(1)} %convert.3, f32[4,256]{0,1:T(8,128)S(1)} %copy.55), kind=kLoop, calls=%fused_computation.10 | loop fusion | flops 1572864 | bytes 4722688 | tf_op jit(solution)/shard_map/convert_element_type | solution.py:76
  44.6 10.6 %all-to-all-done = bf16[4,256,768]{2,0,1:T(4,128)(2,1)} async-done(((bf16[4,256,768]{2,0,1:T(4,128)(2,1)}), bf16[4,256,768]{2,0,1:T(4,128)(2,1)}, u32[]{:S(2)}, u32[]{:S(2)}) %all-to-all-start) | async-done | bytes 1572896 | tf_op jit(solution)/shard_map/all_to_all | solution.py:78
  55.1 4.3 %all-to-all-start.2 = ((bf16[4,256,768]{2,0,1:T(4,128)(2,1)}), bf16[4,256,768]{2,0,1:T(4,128)(2,1)}, u32[]{:S(2)}, u32[]{:S(2)}) async-start(bf16[4,256,768]{2,0,1:T(4,128)(2,1)} %fusion), calls=%async_computation.2 | async-start | bytes 3145728 | tf_op jit(solution)/shard_map/all_to_all | solution.py:81
  59.4 0.2 reduce-scatter.8.cloned.1.call-start
  59.7 3.8 %copy.60 = bf16[4,256,768]{1,2,0:T(8,128)(2,1)} copy(bf16[4,256,768]{2,0,1:T(4,128)(2,1)} %all-to-all-done) | data formatting | bytes 3145728 | tf_op jit(solution)/shard_map/all_to_all | solution.py:78
  63.4 4.5 %fusion.15 = f32[4,256,384]{2,1,0:T(8,128)} fusion(bf16[4,256,768]{1,2,0:T(8,128)(2,1)} %copy.60, bf16[4,768,384]{2,1,0:T(8,128)(2,1)} %param.12), kind=kOutput, calls=%fused_computation.55 | convolution fusion | flops 603979776 | bytes 5505024 | tf_op jit(solution)/shard_map/erd,edf->erf/dot_general | solution.py:9
  67.9 2.2 fusion.14
  70.1 9.4 %all-to-all-done.2 = bf16[4,256,768]{2,0,1:T(4,128)(2,1)} async-done(((bf16[4,256,768]{2,0,1:T(4,128)(2,1)}), bf16[4,256,768]{2,0,1:T(4,128)(2,1)}, u32[]{:S(2)}, u32[]{:S(2)}) %all-to-all-start.2) | async-done | bytes 1572896 | tf_op jit(solution)/shard_map/all_to_all | solution.py:81
  79.6 3.8 %copy.62 = bf16[4,256,768]{1,2,0:T(8,128)(2,1)} copy(bf16[4,256,768]{2,0,1:T(4,128)(2,1)} %all-to-all-done.2) | data formatting | bytes 3145728 | tf_op jit(solution)/shard_map/all_to_all | solution.py:81
  83.3 4.8 %multiply_convert_fusion.3 = (bf16[4,256,384]{2,1,0:T(8,128)(2,1)}, bf16[4,256,384]{2,1,0:T(8,128)(2,1)S(1)}, bf16[4,256,384]{2,1,0:T(8,128)(2,1)S(1)}) fusion(f32[4,256,384]{2,1,0:T(8,128)} %fusion.14, f32[4,256,384]{2,1,0:T(8,128)} %fusion.15, bf16[4,256,768]{1,2,0:T(8,128)(2,1)} %copy.62, bf16[4,768,384]{2,1,0:T(8,128)(2,1)S(1)} %copy-done), kind=kOutput, calls=%fused_computation.14 | convolution fusion | flops 609878016 | bytes 9437184 | tf_op jit(solution)/shard_map/erd,edf->erf/dot_general | solution.py:21
  88.2 1.0 copy-done.7
  89.2 2.4 multiply_convert_fusion
  91.6 0.0 reduce-scatter.8.cloned.1.call-update
  91.6 0.0 reduce-scatter.6.cloned.1.call-start
  91.7 4.0 %multiply_convert_fusion.1 = bf16[4,768,384]{2,1,0:T(8,128)(2,1)} fusion(bf16[4,256,768]{1,2,0:T(8,128)(2,1)} %copy.60, bf16[4,256,384]{2,1,0:T(8,128)(2,1)} %get-tuple-element.7), kind=kOutput, calls=%fused_computation.7 | convolution fusion | flops 606339072 | bytes 4718592 | tf_op jit(solution)/shard_map/erd,erf->edf/dot_general | solution.py:35
  95.6 0.0 reduce-scatter.6.cloned.1.call-update
  95.7 0.0 reduce-scatter.4.cloned.1.call-start
  95.7 3.8 %multiply_convert_fusion.2 = bf16[4,768,384]{2,1,0:T(8,128)(2,1)} fusion(bf16[4,256,768]{1,2,0:T(8,128)(2,1)} %copy.60, bf16[4,256,384]{2,1,0:T(8,128)(2,1)S(1)} %get-tuple-element.8), kind=kOutput, calls=%fused_computation.8 | convolution fusion | flops 606339072 | bytes 4718592 | tf_op jit(solution)/shard_map/erd,erf->edf/dot_general | solution.py:31
  99.5 0.0 reduce-scatter.4.cloned.1.call-update
  99.6 2.2 convolution_convert_fusion
  101.7 2.4 copy.52
  104.1 4.4 %all-to-all-start.1 = ((bf16[4,256,768]{2,0,1:T(4,128)(2,1)}), bf16[4,256,768]{2,0,1:T(4,128)(2,1)}, u32[]{:S(2)}, u32[]{:S(2)}) async-start(bf16[4,256,768]{2,0,1:T(4,128)(2,1)} %copy.52), calls=%async_computation.1 | async-start | bytes 3145728 | tf_op jit(solution)/shard_map/all_to_all | solution.py:80
  108.5 0.0 copy-start.5
  108.5 2.8 fusion.16
  111.4 1.0 add_convert_fusion
  112.4 2.4 copy.58
  114.8 13.8 %all-to-all-done.1 = bf16[4,256,768]{2,0,1:T(4,128)(2,1)} async-done(((bf16[4,256,768]{2,0,1:T(4,128)(2,1)}), bf16[4,256,768]{2,0,1:T(4,128)(2,1)}, u32[]{:S(2)}, u32[]{:S(2)}) %all-to-all-start.1) | async-done | bytes 1572896 | tf_op jit(solution)/shard_map/all_to_all | solution.py:80
  128.6 4.6 %all-to-all-start.3 = ((bf16[4,256,768]{2,0,1:T(4,128)(2,1)}), bf16[4,256,768]{2,0,1:T(4,128)(2,1)}, u32[]{:S(2)}, u32[]{:S(2)}) async-start(bf16[4,256,768]{2,0,1:T(4,128)(2,1)} %copy.58), calls=%async_computation.3 | async-start | bytes 3145728 | tf_op jit(solution)/shard_map/all_to_all | solution.py:85
  133.2 2.9 copy.53
  136.1 4.0 %gather_fusion.1 = bf16[512,768]{1,0:T(8,128)(2,1)S(1)} fusion(bf16[1024,768]{1,0:T(8,128)(2,1)} %bitcast.42, s32[1024]{0:T(1024)S(1)} %pad_clamp_fusion), kind=kCustom, calls=%fused_computation.1 | custom fusion | bytes 1574912 | tf_op jit(solution)/shard_map/gather | solution.py:88
  140.1 2.0 reshape.200
  142.0 11.3 %all-to-all-done.3 = bf16[4,256,768]{2,0,1:T(4,128)(2,1)} async-done(((bf16[4,256,768]{2,0,1:T(4,128)(2,1)}), bf16[4,256,768]{2,0,1:T(4,128)(2,1)}, u32[]{:S(2)}, u32[]{:S(2)}) %all-to-all-start.3) | async-done | bytes 1572896 | tf_op jit(solution)/shard_map/all_to_all | solution.py:85
  153.3 2.8 copy.59
  156.1 4.7 %gather_fusion.4 = bf16[512,768]{1,0:T(8,128)(2,1)} fusion(bf16[1024,768]{1,0:T(8,128)(2,1)} %bitcast.41, s32[1024]{0:T(1024)S(1)} %pad_clamp_fusion), kind=kCustom, calls=%fused_computation.4 | custom fusion | bytes 1574912 | tf_op jit(solution)/shard_map/gather | solution.py:88
  160.8 2.2 gather.25
  162.9 2.8 reduce_sum.35
  165.8 4.2 %multiply_reduce_fusion = bf16[256,768]{1,0:T(8,128)(2,1)} fusion(f32[256,2,768]{2,1,0:T(2,128)} %reshape.200, f32[256,2]{1,0:T(8,128)S(1)} %copy.43), kind=kLoop, calls=%fused_computation.16 | loop fusion | flops 589824 | bytes 1968128 | tf_op jit(solution)/shard_map/reduce_sum | solution.py:89
  169.9 1.8 convert_element_type.88
  171.7 63.0 %reduce-scatter.6.cloned.1.call-done = bf16[4,96,384]{2,1,0:T(8,128)(2,1)} async-done(((bf16[4,768,384]{2,1,0:T(8,128)(2,1)}), bf16[4,96,384]{2,1,0:T(8,128)(2,1)}) %reduce-scatter.6.cloned.1.call-update) | async-done | bytes 294928 | tf_op jit(solution)/shard_map/reduce_scatter | solution.py:98
  234.8 1.8 convert_element_type.86
  236.6 70.9 %reduce-scatter.4.cloned.1.call-done = bf16[4,96,384]{2,1,0:T(8,128)(2,1)} async-done(((bf16[4,768,384]{2,1,0:T(8,128)(2,1)}), bf16[4,96,384]{2,1,0:T(8,128)(2,1)}) %reduce-scatter.4.cloned.1.call-update) | async-done | bytes 294928 | tf_op jit(solution)/shard_map/reduce_scatter | solution.py:95
  307.5 1.8 convert_element_type.84
  (25 shorter events, 0.2 us)
Async XLA Ops:
  7.2 76.2 %copy-start = (bf16[4,768,384]{2,1,0:T(8,128)(2,1)S(1)}, bf16[4,768,384]{2,1,0:T(8,128)(2,1)}, u32[]{:S(2)}) copy-start(bf16[4,768,384]{2,1,0:T(8,128)(2,1)} %param.13) | copy-start | bytes 7077892
  13.6 7.1 %copy-start.1 = (bf16[256,768]{1,0:T(8,128)(2,1)S(1)}, bf16[256,768]{1,0:T(8,128)(2,1)}, u32[]{:S(2)}) copy-start(bf16[256,768]{1,0:T(8,128)(2,1)} %param.7) | copy-start | bytes 1179652
  29.8 4.6 %copy-start.2 = (bf16[256,768]{1,0:T(8,128)(2,1)S(1)}, bf16[256,768]{1,0:T(8,128)(2,1)}, u32[]{:S(2)}) copy-start(bf16[256,768]{1,0:T(8,128)(2,1)} %param.10) | copy-start | bytes 1179652
  29.8 25.3 %all-to-all-start = ((bf16[4,256,768]{2,0,1:T(4,128)(2,1)}), bf16[4,256,768]{2,0,1:T(4,128)(2,1)}, u32[]{:S(2)}, u32[]{:S(2)}) async-start(bf16[4,256,768]{2,0,1:T(4,128)(2,1)} %copy_select_fusion), calls=%async_computation | async-start | bytes 3145728 | tf_op jit(solution)/shard_map/all_to_all | solution.py:78
  55.1 24.5 %all-to-all-start.2 = ((bf16[4,256,768]{2,0,1:T(4,128)(2,1)}), bf16[4,256,768]{2,0,1:T(4,128)(2,1)}, u32[]{:S(2)}, u32[]{:S(2)}) async-start(bf16[4,256,768]{2,0,1:T(4,128)(2,1)} %fusion), calls=%async_computation.2 | async-start | bytes 3145728 | tf_op jit(solution)/shard_map/all_to_all | solution.py:81
  59.4 110.5 %reduce-scatter.8.cloned.1.call-start = ((), (), s32[]{:S(2)}) async-start(), calls=%async_computation.9 | async-start | bytes 2654208 | tf_op jit(solution)/shard_map/reduce_scatter | solution.py:101
  63.4 4.5 %copy-start.3 = (bf16[4,256,768]{1,2,0:T(8,128)(2,1)S(1)}, bf16[4,256,768]{1,2,0:T(8,128)(2,1)}, u32[]{:S(2)}) copy-start(bf16[4,256,768]{1,2,0:T(8,128)(2,1)} %copy.60) | copy-start | bytes 4718596
  63.4 4.5 %copy-start.4 = (bf16[4,768,384]{2,1,0:T(8,128)(2,1)S(1)}, bf16[4,768,384]{2,1,0:T(8,128)(2,1)}, u32[]{:S(2)}) copy-start(bf16[4,768,384]{2,1,0:T(8,128)(2,1)} %param.11) | copy-start | bytes 7077892
  83.3 5.8 %copy-start.6 = (bf16[4,256,768]{1,2,0:T(8,128)(2,1)S(1)}, bf16[4,256,768]{1,2,0:T(8,128)(2,1)}, u32[]{:S(2)}) copy-start(bf16[4,256,768]{1,2,0:T(8,128)(2,1)} %copy.62) | copy-start | bytes 4718596
  88.2 1.0 copy-start.7
  91.6 143.2 %reduce-scatter.6.cloned.1.call-start = ((), (), s32[]{:S(2)}) async-start(), calls=%async_computation.8 | async-start | bytes 2654208 | tf_op jit(solution)/shard_map/reduce_scatter | solution.py:98
  95.7 211.9 %reduce-scatter.4.cloned.1.call-start = ((), (), s32[]{:S(2)}) async-start(), calls=%async_computation.7 | async-start | bytes 2654208 | tf_op jit(solution)/shard_map/reduce_scatter | solution.py:95
  104.1 24.5 %all-to-all-start.1 = ((bf16[4,256,768]{2,0,1:T(4,128)(2,1)}), bf16[4,256,768]{2,0,1:T(4,128)(2,1)}, u32[]{:S(2)}, u32[]{:S(2)}) async-start(bf16[4,256,768]{2,0,1:T(4,128)(2,1)} %copy.52), calls=%async_computation.1 | async-start | bytes 3145728 | tf_op jit(solution)/shard_map/all_to_all | solution.py:80
  108.5 2.9 copy-start.5
  108.5 2.9 copy-start.8
  128.6 24.7 %all-to-all-start.3 = ((bf16[4,256,768]{2,0,1:T(4,128)(2,1)}), bf16[4,256,768]{2,0,1:T(4,128)(2,1)}, u32[]{:S(2)}, u32[]{:S(2)}) async-start(bf16[4,256,768]{2,0,1:T(4,128)(2,1)} %copy.58), calls=%async_computation.3 | async-start | bytes 3145728 | tf_op jit(solution)/shard_map/all_to_all | solution.py:85
Sparse Core Ops, SparseCore 0:
  91.7 70.6 reduce-scatter.7
  166.0 68.7 reduce-scatter.5
  238.3 69.1 reduce-scatter.3
where the time goes:
time: 317 us; the launch traced here: 316 us
  waiting for transfers between devices  179 us (56%)
  local copies, waits for them, and re-layouts  53.7 us (17%)
  matrix products  27.8 us (9%)
  other arithmetic  23.2 us (7%)
  starting transfers between devices  18 us (6%)
  between operations  14 us (4%)
    reduce_scatter x1, waiting for transfers between devices, shards(): lax.psum_scatter(weight_gate.astype(jnp.bfloat16), 'dp', scatter_dimensio...  70.9 us
    reduce_scatter x1, waiting for transfers between devices, shards(): lax.psum_scatter(weight_up.astype(jnp.bfloat16), 'dp', scatter_dimension=...  63 us
    all_to_all x1, waiting for transfers between devices, shards(): lax.all_to_all(outputs, 'expert', split_axis=1, concat_axis=1, tiled=True)  13.8 us
    all_to_all x1, waiting for transfers between devices, shards(): lax.all_to_all(entry_grad, 'expert', split_axis=1, concat_axis=1, tiled=T...  11.3 us
    gather x3, local copies, waits for them, and re-layouts, combine(): returned.reshape(slots_all, d_model)[slot_index].astype(jnp.float32)  10.8 us
    all_to_all x1, waiting for transfers between devices, shards(): lax.all_to_all(send_rows, 'expert', split_axis=1, concat_axis=1, tiled=True)  10.6 us
    all_to_all x1, waiting for transfers between devices, shards(): lax.all_to_all(send_grads, 'expert', split_axis=1, concat_axis=1, tiled=T...  9.44 us
    reduce_sum x2, other arithmetic, combine(): jnp.sum((weights[:, None] * picked).reshape(tok_rows, top_count, d_model)...  7 us
  transfers between devices with their start and end apart: 7, of which 6 were waited for; matrix products, arithmetic and copies ran while one was open for 22% of the time, Pallas kernels for 0%

commit v1 on v0

--- a/solution.py
+++ b/solution.py
@@ -2,6 +2,17 @@
 import jax.numpy as jnp
 from jax import lax
 from jax.sharding import PartitionSpec as P
+
+
+def split_up(x, dim, size):
+    before, after = (x.shape[:dim], x.shape[dim + 1 :])
+    return jnp.moveaxis(x.reshape(*before, size, -1, *after), dim, 0)
+
+
+def joined_along(blocks, dim):
+    blocks = jnp.moveaxis(blocks, 0, dim)
+    shape = blocks.shape
+    return blocks.reshape(*shape[:dim], shape[dim] * shape[dim + 1], *shape[dim + 2 :])
 
 
 def expert_forward(rows_in, w_gate, w_up, w_down):
@@ -75,7 +86,15 @@
     send_rows = send_rows.reshape(local_experts, peer_count * capacity, d_model)
     send_grads = (slot_gate[:, None] * cotangent[token_of].astype(jnp.float32)).astype(jnp.bfloat16)
     send_grads = send_grads.reshape(local_experts, peer_count * capacity, d_model)
-    rows_in = lax.all_to_all(send_rows, "expert", split_axis=1, concat_axis=1, tiled=True)
+    size, index = (lax.axis_size("expert"), lax.axis_index("expert"))
+    tiles = split_up(send_rows, 1, size)
+    out = tiles
+    for step in range(1, size):
+        target, source_2 = ((index + step) % size, (index - step) % size)
+        sent = lax.dynamic_index_in_dim(tiles, target, 0)
+        other = lax.ppermute(sent, "expert", [(i, (i + step) % size) for i in range(size)])
+        out = lax.dynamic_update_slice_in_dim(out, other, source_2, axis=0)
+    rows_in = joined_along(out, 1)
     outputs, saved_state = expert_forward(rows_in, w_gate, w_up, w_down)
     back_out = lax.all_to_all(outputs, "expert", split_axis=1, concat_axis=1, tiled=True)
     grads_in = lax.all_to_all(send_grads, "expert", split_axis=1, concat_axis=1, tiled=True)

time: 317 us -> 318 us (level)
  matrix products: 27.8 us -> 24.5 us
  local copies, waits for them, and re-layouts: 53.7 us -> 56.9 us
    ppermute x0 -> x3, waiting for transfers between devices: none -> 21.9 us  [shards(): lax.ppermute(sent, 'expert', [(i, (i + step) % size) for i in range(size)])]
    all_to_all x1 -> x0, waiting for transfers between devices: 10.6 us -> none  [shards(): lax.all_to_all(send_rows, 'expert', split_axis=1, concat_axis=1, tiled=True)]
    all_to_all x1, waiting for transfers between devices: 9.44 us -> 0.01 us  [shards(): lax.all_to_all(send_grads, 'expert', split_axis=1, concat_axis=1, tiled=T...]
    dynamic_update_slice x0 -> x3, local copies, waits for them, and re-layouts: none -> 5.32 us  [shards(): out = lax.dynamic_update_slice_in_dim(out, other, source_2, axis=0)]
    ppermute x0 -> x3, starting transfers between devices: none -> 4.72 us  [shards(): lax.ppermute(sent, 'expert', [(i, (i + step) % size) for i in range(size)])]
    all_to_all x1 -> x0, starting transfers between devices: 4.47 us -> none  [shards(): lax.all_to_all(send_rows, 'expert', split_axis=1, concat_axis=1, tiled=True)]
    all_to_all x1 -> x0, local copies, waits for them, and re-layouts: 3.76 us -> none  [shards(): lax.all_to_all(send_rows, 'expert', split_axis=1, concat_axis=1, tiled=True)]
  transfers between devices with their start and end apart: 7 -> 9, of which waited for: 6 -> 6; matrix products, arithmetic and copies ran while one was open for 22% -> 20% of each run, Pallas kernels for 0% -> 0%
where the time goes in v1:
time: 318 us; the launch traced here: 317 us
  waiting for transfers between devices  180 us (57%)
  local copies, waits for them, and re-layouts  56.9 us (18%)
  matrix products  24.5 us (8%)
  other arithmetic  22.5 us (7%)
  starting transfers between devices  18.5 us (6%)
  between operations  14.1 us (4%)
    reduce_scatter x1, waiting for transfers between devices, shards(): lax.psum_scatter(weight_gate.astype(jnp.bfloat16), 'dp', scatter_dimensio...  70.5 us
    reduce_scatter x1, waiting for transfers between devices, shards(): lax.psum_scatter(weight_up.astype(jnp.bfloat16), 'dp', scatter_dimension=...  62.1 us
    ppermute x3, waiting for transfers between devices, shards(): lax.ppermute(sent, 'expert', [(i, (i + step) % size) for i in range(size)])  21.9 us
    all_to_all x1, waiting for transfers between devices, shards(): lax.all_to_all(outputs, 'expert', split_axis=1, concat_axis=1, tiled=True)  14.8 us
    all_to_all x1, waiting for transfers between devices, shards(): lax.all_to_all(entry_grad, 'expert', split_axis=1, concat_axis=1, tiled=T...  11 us
    gather x3, local copies, waits for them, and re-layouts, combine(): returned.reshape(slots_all, d_model)[slot_index].astype(jnp.float32)  10.9 us
    reduce_sum x2, other arithmetic, combine(): jnp.sum((weights[:, None] * picked).reshape(tok_rows, top_count, d_model)...  7 us
    gather x1, local copies, waits for them, and re-layouts, shards(): gate_values[jnp.minimum(source, entries - 1)]  6.87 us
  transfers between devices with their start and end apart: 9, of which 6 were waited for; matrix products, arithmetic and copies ran while one was open for 20% of the time, Pallas kernels for 0%

profile of v1, /device:TPU:0, one launch (start us, length us, event | category | flops | bytes accessed | tf_op | source)
XLA Modules:
  0.0 316.8 jit_solution(5948813317614649762)
XLA Ops:
  7.2 1.0 copy.42
  8.1 0.1 eq.38
  8.3 0.1 eq.34
  8.4 0.1 reshape.201
  8.6 0.7 convert_multiply_fusion
  9.3 0.1 copy.41
  9.4 0.1 div.43
  9.6 1.2 reduce-window.6
  10.7 0.2 slice_reduce_fusion
  11.0 0.1 fusion.3
  11.1 2.4 scatter_custom_fusion
  13.6 6.9 %gather_fusion.2 = f32[1024]{0:T(1024)S(1)} fusion(f32[512]{0:T(512)S(1)} %div.43, s32[1024]{0:T(1024)S(1)} %fusion.8), kind=kCustom, calls=%fused_computation.2 | custom fusion | bytes 12288 | tf_op jit(solution)/shard_map/gather | solution.py:84
  20.5 0.1 copy.49
  20.7 5.2 %gather_fusion.3 = bf16[1024,768]{1,0:T(8,128)(2,1)} fusion(bf16[256,768]{1,0:T(8,128)(2,1)S(1)} %copy-done.1, s32[1024]{0:T(1024)S(1)} %fusion.7), kind=kCustom, calls=%fused_computation.3 | custom fusion | bytes 3149824 | tf_op jit(solution)/shard_map/gather | solution.py:87
  25.9 1.7 convert.3
  27.6 3.3 %fusion = bf16[4,256,768]{2,0,1:T(4,128)(2,1)} fusion(f32[4,256,768]{2,1,0:T(8,128)S(1)} %convert.3, f32[4,256]{0,1:T(8,128)S(1)} %copy.49), kind=kLoop, calls=%fused_computation.10 | loop fusion | flops 1572864 | bytes 4722688 | tf_op jit(solution)/shard_map/convert_element_type | solution.py:87
  30.9 4.5 %all-to-all-start.1 = ((bf16[4,256,768]{2,0,1:T(4,128)(2,1)}), bf16[4,256,768]{2,0,1:T(4,128)(2,1)}, u32[]{:S(2)}, u32[]{:S(2)}) async-start(bf16[4,256,768]{2,0,1:T(4,128)(2,1)} %fusion), calls=%async_computation.1 | async-start | bytes 3145728 | tf_op jit(solution)/shard_map/all_to_all | solution.py:100
  35.4 0.1 broadcast_in_dim.34
  35.5 5.2 %gather_fusion = bf16[1024,768]{1,0:T(8,128)(2,1)} fusion(bf16[256,768]{1,0:T(8,128)(2,1)S(1)} %copy-done.2, s32[1024]{0:T(1024)S(1)} %fusion.7), kind=kCustom, calls=%fused_computation | custom fusion | bytes 3149824 | tf_op jit(solution)/shard_map/gather | solution.py:85
  40.8 1.6 broadcast_select_fusion
  42.4 0.8 dynamic-slice_bitcast_fusion
  43.2 0.5 collective-permute-start
  43.7 2.0 collective-permute-start.2
  45.7 2.3 collective-permute-start.1
  47.9 1.4 fusion.35
  49.4 14.4 %collective-permute-done = bf16[1,4,64,768]{3,2,0,1:T(8,128)(2,1)} collective-permute-done((bf16[1,4,64,768]{3,2,0,1:T(8,128)(2,1)}, bf16[1,4,64,768]{3,2,0,1:T(8,128)(2,1)}, u32[]{:S(2)}, u32[]{:S(2)}) %collective-permute-start) | collective-permute-done | bytes 393248 | tf_op jit(solution)/shard_map/ppermute | solution.py:95
  63.8 1.8 constant_dynamic-update-slice_fusion.2
  65.5 7.5 %collective-permute-done.1 = bf16[1,4,64,768]{3,2,0,1:T(8,128)(2,1)} collective-permute-done((bf16[1,4,64,768]{3,2,0,1:T(8,128)(2,1)S(1)}, bf16[1,4,64,768]{3,2,0,1:T(8,128)(2,1)}, u32[]{:S(2)}, u32[]{:S(2)}) %collective-permute-start.1) | collective-permute-done | bytes 393248 | tf_op jit(solution)/shard_map/ppermute | solution.py:95
  73.0 1.8 constant_dynamic-update-slice_fusion.1
  74.8 1.8 constant_dynamic-update-slice_fusion
  76.6 3.5 %fusion.14 = f32[4,256,384]{2,1,0:T(8,128)} fusion(bf16[4,256,768]{2,1,0:T(8,128)(2,1)} %bitcast.54, bf16[4,768,384]{2,1,0:T(8,128)(2,1)S(1)} %copy-done.5), kind=kOutput, calls=%fused_computation.60 | convolution fusion | flops 603979776 | bytes 5505024 | tf_op jit(solution)/shard_map/erd,edf->erf/dot_general | solution.py:20
  80.1 3.8 %copy.56 = bf16[4,256,768]{1,2,0:T(8,128)(2,1)} copy(bf16[4,256,768]{2,0,1:T(4,128)(2,1)} %all-to-all-done.1) | data formatting | bytes 3145728 | tf_op jit(solution)/shard_map/all_to_all | solution.py:100
  83.9 3.3 %fusion.15 = f32[4,256,384]{2,1,0:T(8,128)S(1)} fusion(bf16[4,256,768]{1,2,0:T(8,128)(2,1)} %copy.56, bf16[4,768,384]{2,1,0:T(8,128)(2,1)} %param.13), kind=kOutput, calls=%fused_computation.61 | convolution fusion | flops 603979776 | bytes 5505024 | tf_op jit(solution)/shard_map/erd,edf->erf/dot_general | solution.py:32
  87.3 2.3 multiply_convert_fusion.3
  89.6 1.0 copy-done.10
  90.5 2.4 multiply_convert_fusion
  93.0 0.2 reduce-scatter.6.cloned.1.call-start
  93.2 4.0 %multiply_convert_fusion.1 = bf16[4,768,384]{2,1,0:T(8,128)(2,1)} fusion(bf16[4,256,768]{2,1,0:T(8,128)(2,1)} %bitcast.55, bf16[4,256,384]{2,1,0:T(8,128)(2,1)} %get-tuple-element.7), kind=kOutput, calls=%fused_computation.7 | convolution fusion | flops 606339072 | bytes 4718592 | tf_op jit(solution)/shard_map/erd,erf->edf/dot_general | solution.py:46
  97.3 0.0 reduce-scatter.4.cloned.1.call-start
  97.4 3.9 %multiply_convert_fusion.2 = bf16[4,768,384]{2,1,0:T(8,128)(2,1)} fusion(bf16[4,256,768]{2,1,0:T(8,128)(2,1)} %bitcast.56, bf16[4,256,384]{2,1,0:T(8,128)(2,1)S(1)} %get-tuple-element.8), kind=kOutput, calls=%fused_computation.8 | convolution fusion | flops 606339072 | bytes 4718592 | tf_op jit(solution)/shard_map/erd,erf->edf/dot_general | solution.py:42
  101.2 2.9 convolution_convert_fusion
  104.2 2.4 copy.46
  106.6 4.4 %all-to-all-start = ((bf16[4,256,768]{2,0,1:T(4,128)(2,1)}), bf16[4,256,768]{2,0,1:T(4,128)(2,1)}, u32[]{:S(2)}, u32[]{:S(2)}) async-start(bf16[4,256,768]{2,0,1:T(4,128)(2,1)} %copy.46), calls=%async_computation | async-start | bytes 3145728 | tf_op jit(solution)/shard_map/all_to_all | solution.py:99
  111.0 1.0 fusion.16
  112.0 0.7 copy-done.6
  112.7 0.2 copy-done.8
  112.9 1.0 add_convert_fusion
  113.9 2.4 copy.52
  116.3 14.8 %all-to-all-done = bf16[4,256,768]{2,0,1:T(4,128)(2,1)} async-done(((bf16[4,256,768]{2,0,1:T(4,128)(2,1)}), bf16[4,256,768]{2,0,1:T(4,128)(2,1)}, u32[]{:S(2)}, u32[]{:S(2)}) %all-to-all-start) | async-done | bytes 1572896 | tf_op jit(solution)/shard_map/all_to_all | solution.py:99
  131.1 4.6 %all-to-all-start.2 = ((bf16[4,256,768]{2,0,1:T(4,128)(2,1)}), bf16[4,256,768]{2,0,1:T(4,128)(2,1)}, u32[]{:S(2)}, u32[]{:S(2)}) async-start(bf16[4,256,768]{2,0,1:T(4,128)(2,1)} %copy.52), calls=%async_computation.2 | async-start | bytes 3145728 | tf_op jit(solution)/shard_map/all_to_all | solution.py:104
  135.7 2.9 copy.47
  138.6 4.0 %gather_fusion.1 = bf16[512,768]{1,0:T(8,128)(2,1)S(1)} fusion(bf16[1024,768]{1,0:T(8,128)(2,1)} %bitcast.53, s32[1024]{0:T(1024)S(1)} %pad_clamp_fusion), kind=kCustom, calls=%fused_computation.1 | custom fusion | bytes 1574912 | tf_op jit(solution)/shard_map/gather | solution.py:107
  142.6 2.0 reshape.206
  144.6 11.0 %all-to-all-done.2 = bf16[4,256,768]{2,0,1:T(4,128)(2,1)} async-done(((bf16[4,256,768]{2,0,1:T(4,128)(2,1)}), bf16[4,256,768]{2,0,1:T(4,128)(2,1)}, u32[]{:S(2)}, u32[]{:S(2)}) %all-to-all-start.2) | async-done | bytes 1572896 | tf_op jit(solution)/shard_map/all_to_all | solution.py:104
  155.6 2.8 copy.53
  158.3 4.7 %gather_fusion.4 = bf16[512,768]{1,0:T(8,128)(2,1)} fusion(bf16[1024,768]{1,0:T(8,128)(2,1)} %bitcast.52, s32[1024]{0:T(1024)S(1)} %pad_clamp_fusion), kind=kCustom, calls=%fused_computation.4 | custom fusion | bytes 1574912 | tf_op jit(solution)/shard_map/gather | solution.py:107
  163.0 2.2 gather.25
  165.2 2.8 reduce_sum.35
  168.0 4.2 %multiply_reduce_fusion = bf16[256,768]{1,0:T(8,128)(2,1)} fusion(f32[256,2,768]{2,1,0:T(2,128)} %reshape.206, f32[256,2]{1,0:T(8,128)S(1)} %copy.41), kind=kLoop, calls=%fused_computation.15 | loop fusion | flops 589824 | bytes 1968128 | tf_op jit(solution)/shard_map/reduce_sum | solution.py:108
  172.2 1.8 convert_element_type.88
  174.0 62.1 %reduce-scatter.6.cloned.1.call-done = bf16[4,96,384]{2,1,0:T(8,128)(2,1)} async-done(((bf16[4,768,384]{2,1,0:T(8,128)(2,1)}), bf16[4,96,384]{2,1,0:T(8,128)(2,1)}) %reduce-scatter.6.cloned.1.call-update) | async-done | bytes 294928 | tf_op jit(solution)/shard_map/reduce_scatter | solution.py:117
  236.2 1.8 convert_element_type.86
  238.0 70.5 %reduce-scatter.4.cloned.1.call-done = bf16[4,96,384]{2,1,0:T(8,128)(2,1)} async-done(((bf16[4,768,384]{2,1,0:T(8,128)(2,1)}), bf16[4,96,384]{2,1,0:T(8,128)(2,1)}) %reduce-scatter.4.cloned.1.call-update) | async-done | bytes 294928 | tf_op jit(solution)/shard_map/reduce_scatter | solution.py:114
  308.5 1.8 convert_element_type.84
  (36 shorter events, 0.3 us)
Async XLA Ops:
  7.2 80.0 %copy-start = (bf16[4,768,384]{2,1,0:T(8,128)(2,1)S(1)}, bf16[4,768,384]{2,1,0:T(8,128)(2,1)}, u32[]{:S(2)}) copy-start(bf16[4,768,384]{2,1,0:T(8,128)(2,1)} %param.11) | copy-start | bytes 7077892
  13.6 7.1 %copy-start.1 = (bf16[256,768]{1,0:T(8,128)(2,1)S(1)}, bf16[256,768]{1,0:T(8,128)(2,1)}, u32[]{:S(2)}) copy-start(bf16[256,768]{1,0:T(8,128)(2,1)} %param.10) | copy-start | bytes 1179652
  30.9 4.7 %copy-start.2 = (bf16[256,768]{1,0:T(8,128)(2,1)S(1)}, bf16[256,768]{1,0:T(8,128)(2,1)}, u32[]{:S(2)}) copy-start(bf16[256,768]{1,0:T(8,128)(2,1)} %param.7) | copy-start | bytes 1179652
  30.9 49.3 %all-to-all-start.1 = ((bf16[4,256,768]{2,0,1:T(4,128)(2,1)}), bf16[4,256,768]{2,0,1:T(4,128)(2,1)}, u32[]{:S(2)}, u32[]{:S(2)}) async-start(bf16[4,256,768]{2,0,1:T(4,128)(2,1)} %fusion), calls=%async_computation.1 | async-start | bytes 3145728 | tf_op jit(solution)/shard_map/all_to_all | solution.py:100
  35.4 136.8 %reduce-scatter.8.cloned.1.call-start = ((), (), s32[]{:S(2)}) async-start(), calls=%async_computation.8 | async-start | bytes 2654208 | tf_op jit(solution)/shard_map/reduce_scatter | solution.py:120
  42.4 5.6 %copy-start.4 = (bf16[1024,768]{1,0:T(8,128)(2,1)S(1)}, bf16[1024,768]{1,0:T(8,128)(2,1)}, u32[]{:S(2)}) copy-start(bf16[1024,768]{1,0:T(8,128)(2,1)} %gather_fusion) | copy-start | bytes 4718596
  43.2 20.5 %collective-permute-start = (bf16[1,4,64,768]{3,2,0,1:T(8,128)(2,1)}, bf16[1,4,64,768]{3,2,0,1:T(8,128)(2,1)}, u32[]{:S(2)}, u32[]{:S(2)}) collective-permute-start(bf16[1,4,64,768]{3,2,0,1:T(8,128)(2,1)} %get-tuple-element.12), channel_id=1, source_target_pairs={{0,1},{1,2},{2,3},{3,0},{4,5},{5,6},{6,7},{7,4},{8,9},{9,10},{10,1... | collective-permute-start | bytes 1179656 | tf_op jit(solution)/shard_map/ppermute | solution.py:95
  43.7 31.1 %collective-permute-start.2 = (bf16[1,4,64,768]{3,2,0,1:T(8,128)(2,1)S(1)}, bf16[1,4,64,768]{3,2,0,1:T(8,128)(2,1)}, u32[]{:S(2)}, u32[]{:S(2)}) collective-permute-start(bf16[1,4,64,768]{3,2,0,1:T(8,128)(2,1)S(1)} %get-tuple-element.10), channel_id=1, source_target_pairs={{0,3},{1,0},{2,1},{3,2},{4,7},{5,4},{6,5},{7,6},{8,11},{9,8},{10,9... | collective-permute-start | bytes 1179656 | tf_op jit(solution)/shard_map/ppermute | solution.py:95
  45.7 27.4 %collective-permute-start.1 = (bf16[1,4,64,768]{3,2,0,1:T(8,128)(2,1)S(1)}, bf16[1,4,64,768]{3,2,0,1:T(8,128)(2,1)}, u32[]{:S(2)}, u32[]{:S(2)}) collective-permute-start(bf16[1,4,64,768]{3,2,0,1:T(8,128)(2,1)S(1)} %get-tuple-element.11), channel_id=1, source_target_pairs={{0,2},{1,3},{2,0},{3,1},{4,6},{5,7},{6,4},{7,5},{8,10},{9,11},{10,... | collective-permute-start | bytes 1179656 | tf_op jit(solution)/shard_map/ppermute | solution.py:95
  49.4 27.2 %copy-start.5 = (bf16[4,768,384]{2,1,0:T(8,128)(2,1)S(1)}, bf16[4,768,384]{2,1,0:T(8,128)(2,1)}, u32[]{:S(2)}) copy-start(bf16[4,768,384]{2,1,0:T(8,128)(2,1)} %param.12) | copy-start | bytes 7077892
  83.9 3.3 %copy-start.3 = (bf16[4,4,64,768]{3,2,0,1:T(8,128)(2,1)S(1)}, bf16[4,4,64,768]{3,2,0,1:T(8,128)(2,1)}, u32[]{:S(2)}) copy-start(bf16[4,4,64,768]{3,2,0,1:T(8,128)(2,1)} %constant_dynamic-update-slice_fusion) | copy-start | bytes 4718596
  83.9 3.3 %copy-start.9 = (f32[4,256,384]{2,1,0:T(8,128)S(1)}, f32[4,256,384]{2,1,0:T(8,128)}, u32[]{:S(2)}) copy-start(f32[4,256,384]{2,1,0:T(8,128)} %fusion.14) | copy-start | bytes 4718596
  87.2 3.3 %copy-start.7 = (bf16[4,256,768]{1,2,0:T(8,128)(2,1)S(1)}, bf16[4,256,768]{1,2,0:T(8,128)(2,1)}, u32[]{:S(2)}) copy-start(bf16[4,256,768]{1,2,0:T(8,128)(2,1)} %copy.56) | copy-start | bytes 4718596
  89.6 1.0 copy-start.10
  93.0 143.2 %reduce-scatter.6.cloned.1.call-start = ((), (), s32[]{:S(2)}) async-start(), calls=%async_computation.7 | async-start | bytes 2654208 | tf_op jit(solution)/shard_map/reduce_scatter | solution.py:117
  97.3 211.2 %reduce-scatter.4.cloned.1.call-start = ((), (), s32[]{:S(2)}) async-start(), calls=%async_computation.6 | async-start | bytes 2654208 | tf_op jit(solution)/shard_map/reduce_scatter | solution.py:114
  106.6 24.5 %all-to-all-start = ((bf16[4,256,768]{2,0,1:T(4,128)(2,1)}), bf16[4,256,768]{2,0,1:T(4,128)(2,1)}, u32[]{:S(2)}, u32[]{:S(2)}) async-start(bf16[4,256,768]{2,0,1:T(4,128)(2,1)} %copy.46), calls=%async_computation | async-start | bytes 3145728 | tf_op jit(solution)/shard_map/all_to_all | solution.py:99
  111.0 1.7 copy-start.6
  111.0 1.9 copy-start.8
  131.1 24.5 %all-to-all-start.2 = ((bf16[4,256,768]{2,0,1:T(4,128)(2,1)}), bf16[4,256,768]{2,0,1:T(4,128)(2,1)}, u32[]{:S(2)}, u32[]{:S(2)}) async-start(bf16[4,256,768]{2,0,1:T(4,128)(2,1)} %copy.52), calls=%async_computation.2 | async-start | bytes 3145728 | tf_op jit(solution)/shard_map/all_to_all | solution.py:104
Sparse Core Ops, SparseCore 0:
  93.1 70.6 reduce-scatter.7
  167.3 68.8 reduce-scatter.5
  239.7 68.7 reduce-scatter.3
